TPU v7x, 256 devices: a whole 4x4x8 slice. The times are simulated.
256 devices in a mesh: dp: 32 (over z_lo, y, core), tensor: 8 (over x, z_hi).
Axes of the slice: x: 4, y: 4, z: 8 (z_hi: 2, z_lo: 4; z = z_hi * 4 + z_lo), core: 2. Of those that a mesh axis runs over, the one named last changes fastest.
Arguments:
- tokens: bfloat16 [8192, 8192], P(('dp', 'tensor')), may hold values from -6 to 6
- gain: float32 [8192], replicated, may hold values from 0.1 to 1.9
- stale: bfloat16 [8192, 2048], P(None, 'tensor'), may hold values from -0.0625 to 0.0625
- bias: float32 [2048], P('tensor'), may hold values from -3 to 3
- first: float32 [8192, 2048], P(('dp', 'tensor')), may hold values from -6 to 6
- second: float32 [8192, 2048], P(('dp', 'tensor')), may hold values from 0.1 to 10
- grad: float32 [8192, 2048], P(('dp', 'tensor')), may hold values from -6 to 6
- residual: float32 [8192, 2048], P(('dp', 'tensor')), may hold values from -0.12 to 0.12
- exponent: int32 [256, 16], P(('dp', 'tensor')), may hold values from 10 to 17
Outputs:
- new_first: float32 [8192, 2048], P(('dp', 'tensor'))
- new_second: float32 [8192, 2048], P(('dp', 'tensor'))
- projected: bfloat16 [8192, 2048], P('dp', 'tensor')
All inputs are finite; a program needn't handle non-finite values.
Results may differ from a plain program's by a relative error of at most 0.0062.
Values may be sent and summed in bfloat16 or wider, within the bound.
A program may use at most 128 MiB of HBM per device.

v0:
```python
import jax
import jax.numpy as jnp
from jax import lax
from jax.sharding import PartitionSpec as P

QROWS = 32
QCOL = 128


def on_device(tokens, gain, stale, bias, first, second, grad, residual, exponent):
    values = tokens.astype(jnp.float32)
    meansq = jnp.mean(values * values, axis=1, keepdims=True)
    normed = (values * lax.rsqrt(meansq + 1e-06) * gain[None, :]).astype(jnp.bfloat16)
    whole = lax.all_gather(normed, "tensor", axis=0, tiled=True)
    new_first = 0.9 * first + 0.1 * grad
    new_second = 0.95 * second + 0.05 * grad * grad
    corrected = 0.02 * new_first / (jnp.sqrt(new_second) + 1e-08) + residual
    expo = exponent.astype(jnp.float32)
    upward = jnp.exp2(expo)[:, None, :, None]
    downward = jnp.exp2(-expo)[:, None, :, None]
    local_rows = first.shape[0]
    full_cols = first.shape[1]
    blocked = corrected.reshape(exponent.shape[0], QROWS, exponent.shape[1], QCOL) * upward
    quant = jnp.clip(blocked, -448.0, 448.0).astype(jnp.bfloat16)
    quant = lax.optimization_barrier(quant)
    delta = (
        (quant.astype(jnp.float32) * downward).reshape(local_rows, full_cols).astype(jnp.bfloat16)
    )
    head_cols = stale.shape[1]
    gathered = lax.all_gather(delta, "dp", axis=0, tiled=True)
    spread = lax.all_to_all(gathered, "tensor", split_axis=1, concat_axis=0, tiled=True)
    tensor_count = lax.axis_size("tensor")
    replica_count = lax.axis_size("dp")
    ordered = spread.reshape(tensor_count, replica_count, local_rows, head_cols)
    ordered = ordered.transpose(1, 0, 2, 3).reshape(stale.shape[0], head_cols)
    merged = (stale.astype(jnp.float32) + ordered.astype(jnp.float32)).astype(jnp.bfloat16)
    product = jnp.dot(whole, merged, preferred_element_type=jnp.float32)
    projected = (product + bias[None, :]).astype(jnp.bfloat16)
    return (new_first, new_second, projected)


def solution(mesh):
    return jax.shard_map(
        on_device,
        mesh=mesh,
        in_specs=(
            P(("dp", "tensor"), None),
            P(),
            P(None, "tensor"),
            P("tensor"),
            P(("dp", "tensor"), None),
            P(("dp", "tensor"), None),
            P(("dp", "tensor"), None),
            P(("dp", "tensor"), None),
            P(("dp", "tensor"), None),
        ),
        out_specs=(P(("dp", "tensor"), None), P(("dp", "tensor"), None), P("dp", "tensor")),
        check_vma=False,
    )
```

profile of v0, /device:TPU:1, one launch (start us, length us, event | category | flops | bytes accessed | tf_op | source)
XLA Modules:
  0.0 273.7 jit_solution(1441821206613189198)
XLA Ops:
  8.0 0.0 all-gather.5.cloned.1.call-start
  8.0 2.1 add_bitcast_fusion
  10.2 0.7 exponential_bitcast_fusion
  10.9 0.1 fusion.7
  11.0 0.1 multiply_convert_fusion
  11.1 0.7 copy.21
  11.8 0.0 all-gather.5.cloned.1.call-update
  11.8 66.8 %all-gather.5.cloned.1.call-done = bf16[1024,2048]{1,0:T(8,128)(2,1)} async-done(((bf16[32,2048]{1,0:T(8,128)(2,1)}), bf16[1024,2048]{1,0:T(8,128)(2,1)}) %all-gather.5.cloned.1.call-update) | async-done | bytes 4194320 | tf_op jit(solution)/shard_map/all_gather | solution.py:30
  78.6 6.4 %copy.15 = bf16[1024,2048]{0,1:T(8,128)(2,1)} copy(bf16[1024,2048]{1,0:T(8,128)(2,1)} %all-gather.5.cloned.1.call-done) | data formatting | bytes 8388608 | tf_op jit(solution)/shard_map/all_gather | solution.py:30
  85.0 0.0 copy-start.1
  85.0 0.0 copy-start.2
  85.0 7.9 %all-to-all-start = ((bf16[1024,8,256]{0,2,1:T(8,128)(2,1)}), bf16[1024,8,256]{0,2,1:T(8,128)(2,1)}, u32[]{:S(2)}, u32[]{:S(2)}) async-start(bf16[1024,8,256]{0,2,1:T(8,128)(2,1)} %bitcast.32), calls=%async_computation | async-start | bytes 8388608 | tf_op jit(solution)/shard_map/all_to_all | solution.py:31
  92.9 0.0 all-gather.3.cloned.1.call-start
  93.0 0.0 copy-done.1
  93.0 0.2 fusion.2
  93.2 0.0 copy-done.2
  93.2 1.0 fusion.4
  94.2 0.0 all-gather.3.cloned.1.call-update
  94.3 78.9 %all-to-all-done = bf16[1024,8,256]{0,2,1:T(8,128)(2,1)} async-done(((bf16[1024,8,256]{0,2,1:T(8,128)(2,1)}), bf16[1024,8,256]{0,2,1:T(8,128)(2,1)}, u32[]{:S(2)}, u32[]{:S(2)}) %all-to-all-start) | async-done | bytes 4194336 | tf_op jit(solution)/shard_map/all_to_all | solution.py:31
  173.2 6.5 %convert_bitcast_fusion = f32[8,1024,256]{1,2,0:T(8,128)} fusion(bf16[1024,8,256]{0,2,1:T(8,128)(2,1)} %all-to-all-done), kind=kLoop, calls=%fused_computation.2 | loop fusion | flops 2097152 | bytes 12582912 | tf_op jit(solution)/shard_map/convert_element_type | solution.py:36
  179.6 9.1 %copy.16 = f32[8,1024,256]{2,1,0:T(8,128)} copy(f32[8,1024,256]{1,2,0:T(8,128)} %convert_bitcast_fusion) | data formatting | bytes 16777216 | tf_op jit(solution)/shard_map/convert_element_type | solution.py:36
  188.8 0.0 copy-start
  188.8 4.4 %copy.17 = f32[32,8,32,256]{3,2,1,0:T(8,128)S(1)} copy(f32[32,8,32,256]{3,2,0,1:T(8,128)} %bitcast.31) | data formatting | bytes 16777216 | tf_op jit(solution)/shard_map/convert_element_type | solution.py:36
  193.2 0.2 copy-done
  193.4 0.0 copy-start.3
  193.4 3.4 %fusion = bf16[8192,256]{1,0:T(8,128)(2,1)} fusion(f32[32,8,32,256]{3,2,1,0:T(8,128)S(1)} %copy.17, bf16[8192,256]{1,0:T(8,128)(2,1)S(1)} %copy-done), kind=kLoop, calls=%fused_computation.1 | loop fusion | flops 6291456 | bytes 16777216 | tf_op jit(solution)/shard_map/convert_element_type | solution.py:36
  196.8 64.1 %all-gather.3.cloned.1.call-done = bf16[256,8192]{1,0:T(8,128)(2,1)} async-done(((bf16[32,8192]{1,0:T(8,128)(2,1)}), bf16[256,8192]{1,0:T(8,128)(2,1)}) %all-gather.3.cloned.1.call-update) | async-done | bytes 4194320 | tf_op jit(solution)/shard_map/all_gather | solution.py:14
  260.9 0.0 copy-done.3
  260.9 5.4 %fusion.1 = bf16[256,256]{1,0:T(8,128)(2,1)} fusion(bf16[256,8192]{1,0:T(8,128)(2,1)} %all-gather.3.cloned.1.call-done, bf16[8192,256]{1,0:T(8,128)(2,1)} %fusion, f32[256]{0:T(256)S(1)} %copy-done.3), kind=kOutput, calls=%fused_computation.6 | convolution fusion | flops 1073872896 | bytes 8520704 | tf_op jit(solution)/shard_map/dot_general | solution.py:37
  (2 shorter events, 0.1 us)
Async XLA Ops:
  8.0 70.6 %all-gather.5.cloned.1.call-start = ((), (), s32[]{:S(2)}) async-start(), calls=%async_computation.2 | async-start | bytes 4325376 | tf_op jit(solution)/shard_map/all_gather | solution.py:30
  85.0 8.0 %copy-start.1 = (bf16[32,8192]{1,0:T(8,128)(2,1)S(1)}, bf16[32,8192]{1,0:T(8,128)(2,1)}, u32[]{:S(2)}) copy-start(bf16[32,8192]{1,0:T(8,128)(2,1)} %param.9) | copy-start | bytes 1572868
  85.0 8.2 %copy-start.2 = (f32[8192]{0:T(1024)S(1)}, f32[8192]{0:T(1024)}, u32[]{:S(2)}) copy-start(f32[8192]{0:T(1024)} %param.10) | copy-start | bytes 98308
  85.0 88.2 %all-to-all-start = ((bf16[1024,8,256]{0,2,1:T(8,128)(2,1)}), bf16[1024,8,256]{0,2,1:T(8,128)(2,1)}, u32[]{:S(2)}, u32[]{:S(2)}) async-start(bf16[1024,8,256]{0,2,1:T(8,128)(2,1)} %bitcast.32), calls=%async_computation | async-start | bytes 8388608 | tf_op jit(solution)/shard_map/all_to_all | solution.py:31
  92.9 167.9 %all-gather.3.cloned.1.call-start = ((), (), s32[]{:S(2)}) async-start(), calls=%async_computation.1 | async-start | bytes 4718592 | tf_op jit(solution)/shard_map/all_gather | solution.py:14
  188.8 4.6 %copy-start = (bf16[8192,256]{1,0:T(8,128)(2,1)S(1)}, bf16[8192,256]{1,0:T(8,128)(2,1)}, u32[]{:S(2)}) copy-start(bf16[8192,256]{1,0:T(8,128)(2,1)} %param.11) | copy-start | bytes 12582916
  193.4 67.5 %copy-start.3 = (f32[256]{0:T(256)S(1)}, f32[256]{0:T(256)}, u32[]{:S(2)}) copy-start(f32[256]{0:T(256)} %param.12) | copy-start | bytes 3076
Sparse Core Ops, SparseCore 0:
  11.9 66.6 all-gather.4
Sparse Core Ops, SparseCore 1:
  96.0 164.8 all-gather.2
where the time goes:
time: 274 us
  waiting for transfers between devices  210 us (77%)
  local copies, waits for them, and re-layouts  20.8 us (8%)
  between operations  15.5 us (6%)
  other arithmetic  14.1 us (5%)
  starting transfers between devices  7.99 us (3%)
  matrix products  5.37 us (2%)
    all_to_all x1, waiting for transfers between devices, on_device(): lax.all_to_all(gathered, 'tensor', split_axis=1, concat_axis=0, tiled=True)  78.9 us
    all_gather x1, waiting for transfers between devices, on_device(): gathered = lax.all_gather(delta, 'dp', axis=0, tiled=True)  66.8 us
    all_gather x1, waiting for transfers between devices, on_device(): whole = lax.all_gather(normed, 'tensor', axis=0, tiled=True)  64.1 us
    convert_element_type x2, local copies, waits for them, and re-layouts, on_device(): ordered.astype(jnp.float32)  13.5 us
    all_to_all x1, starting transfers between devices, on_device(): lax.all_to_all(gathered, 'tensor', split_axis=1, concat_axis=0, tiled=True)  7.92 us
    convert_element_type x1, other arithmetic, on_device(): ordered.astype(jnp.float32)  6.46 us
    all_gather x1, local copies, waits for them, and re-layouts, on_device(): gathered = lax.all_gather(delta, 'dp', axis=0, tiled=True)  6.38 us
  transfers between devices with their start and end apart: 3, of which 3 were waited for; matrix products, arithmetic and copies ran while one was open for 9% of the time, Pallas kernels for 0%

commit v1 on v0

v1 whole, which is shorter than its diff:
```python
import functools

import jax
import jax.numpy as jnp
from jax import lax
from jax.experimental import pallas as pl
from jax.experimental.pallas import tpu as pltpu
from jax.sharding import PartitionSpec as P

MESH = pl.DeviceIdType.MESH
X, Y, ZL, ZH, C = 4, 4, 4, 2, 2
Z = ZL * ZH
RB = 32
KS = 2048
NB = 512
HC = 256


def ids():
    table, count = {}, 0

    def add(*key):
        nonlocal count
        table[key] = count
        count += 1

    for i in range(1, 8):
        add("stale", i)
    for i in range(1, 4):
        add("y", i)
        add("r", i)
        add("wx", i)
    for p in range(4):
        add("xr", p)
        add("xl", p)
    for p in (0, 3):
        add("fr", p)
    for p in (1, 2):
        add("fl", p)
    for d in range(4):
        for h in range(2):
            add("zr", d, h)
            add("zl", d, h)
    for d in range(5):
        for h in range(2):
            add("sr", d, h)
            add("sl", d, h)
    for b in range(4):
        add("zx", b)
        for dy in range(1, 4):
            add("c", b, dy)
    return table, count


IDS, NIDS = ids()


def kernel(
    tok_ref, gain_ref, stale_ref, first_ref, second_ref, grad_ref, resid_ref, expo_ref,
    out_ref,
    tok, wbuf, sin, delta, wsend, rbuf, rsend, cf, cb, cin, zs, zin, send, recv, loc,
):
    dp = lax.axis_index("dp")
    t = lax.axis_index("tensor")
    c = lax.rem(dp, C)
    y = lax.rem(dp // C, Y)
    zl = dp // (C * Y)
    x = t // ZH
    zh = lax.rem(t, ZH)
    z = zh * ZL + zl

    def at(x_=None, y_=None, z_=None, c_=None):
        x_ = x if x_ is None else x_
        y_ = y if y_ is None else y_
        z_ = z if z_ is None else z_
        c_ = c if c_ is None else c_
        return ((lax.rem(z_, ZL) * Y + y_) * C + c_, x_ * ZH + z_ // ZL)

    xs = [lax.rem(x + i, X) for i in range(X)]
    ys = [lax.rem(y + i, Y) for i in range(Y)]
    zs_ = [lax.rem(z + i, Z) for i in range(Z)]
    ts = [lax.rem(t + i, 8) for i in range(8)]

    def copy(src, dst, dev, *key):
        i = IDS[key]
        return pltpu.make_async_remote_copy(
            src_ref=src, dst_ref=dst, send_sem=send.at[i], recv_sem=recv.at[i],
            device_id=dev, device_id_type=MESH,
        )

    sent = []

    def start(src, dst, dev, *key):
        copy(src, dst, dev, *key).start()
        sent.append((src, dst, dev, key))

    def arrived(ref, *key):
        copy(ref, ref, (dp, t), *key).wait_recv()

    barrier = pltpu.get_barrier_semaphore()
    partners = (
        [(dp, ts[i]) for i in range(1, 8)]
        + [at(y_=ys[i]) for i in range(1, 4)]
        + [at(z_=zs_[1]), at(z_=zs_[7]), at(c_=1 - c)]
    )
    for dev in partners:
        pl.semaphore_signal(barrier, inc=1, device_id=dev, device_id_type=MESH)
    pl.semaphore_wait(barrier, len(partners))

    for i in range(1, 8):
        rows = pl.ds(pl.multiple_of(dp * 256 + ts[i] * RB, RB), RB)
        start(stale_ref.at[rows, :], sin.at[t], (dp, ts[i]), "stale", i)
    rows = pl.ds(pl.multiple_of(dp * 256 + t * RB, RB), RB)
    own_stale = pltpu.make_async_copy(stale_ref.at[rows, :], sin.at[t], loc.at[0])
    own_stale.start()

    def part(k, y_):
        return tok_ref.at[:, pl.ds(pl.multiple_of(k * 2048 + y_ * 512, 512), 512)]

    def spread(dev, y_, *key):
        i = IDS[key]
        for k in range(ZL):
            pltpu.make_async_remote_copy(
                src_ref=part(k, y_), dst_ref=tok.at[x, y, :, pl.ds(k * 512, 512)],
                send_sem=send.at[i], recv_sem=recv.at[i], device_id=dev, device_id_type=MESH,
            ).start()
        sent.append((tok.at[x, y], tok.at[x, y], dev, key))

    spread(at(x_=xs[1]), y, "xr", 0)
    spread(at(x_=xs[3]), y, "xl", 0)
    for dy in (1, 3, 2):
        spread(at(y_=ys[dy]), ys[dy], "y", dy)
    for k in range(ZL):
        pltpu.make_async_copy(part(k, y), tok.at[x, y, :, pl.ds(k * 512, 512)], loc.at[1]).start()

    total = jnp.zeros((RB, 1), jnp.float32)
    for k in range(8):
        v = tok_ref[:, k * 1024:(k + 1) * 1024].astype(jnp.float32)
        total = total + jnp.sum(v * v, axis=1, keepdims=True)
    scale = lax.rsqrt(total / 8192.0 + 1e-06)
    rsend[...] = jnp.broadcast_to(scale, (RB, 128))
    for dx in range(1, 4):
        start(rsend, rbuf.at[dx], at(x_=xs[dx]), "r", dx)

    for j in range(16):
        cols = slice(j * 128, (j + 1) * 128)
        g = grad_ref[:, cols]
        nf = 0.9 * first_ref[:, cols] + 0.1 * g
        ns = 0.95 * second_ref[:, cols] + 0.05 * g * g
        corrected = 0.02 * nf / (jnp.sqrt(ns) + 1e-08) + resid_ref[:, cols]
        e = jnp.broadcast_to(expo_ref[:, j:j + 1], (RB, 128))
        up = lax.shift_left(jnp.ones_like(e), e).astype(jnp.float32)
        down = lax.shift_left(jnp.ones_like(e), 30 - e).astype(jnp.float32) * (2.0 ** -30)
        q = jnp.clip(corrected * up, -448.0, 448.0).astype(jnp.bfloat16)
        delta[:, cols] = q.astype(jnp.float32) * down

    block = dp * 8 + t
    grow = jnp.broadcast_to(gain_ref[pl.ds(block // 4, 1), :], (RB, 128))
    lane = lax.broadcasted_iota(jnp.int32, (RB, 128), 1)
    row = lax.broadcasted_iota(jnp.int32, (RB, 128), 0)
    hit = lane == row + lax.rem(block, 4) * RB
    gcol = jnp.sum(jnp.where(hit, grow, 0.0), axis=1, keepdims=True)

    own_stale.wait()
    for i in range(1, 8):
        arrived(sin.at[lax.rem(t + 8 - i, 8)], "stale", i)
    for tt in range(8):
        w = gcol * (sin[tt].astype(jnp.float32) + delta[:, tt * HC:(tt + 1) * HC])
        wsend[tt // 2, :, (tt % 2) * HC:(tt % 2 + 1) * HC] = w.astype(jnp.bfloat16)
    for dx in range(1, 4):
        start(wsend.at[xs[dx]], wbuf.at[zl, c, x, zh], at(x_=xs[dx]), "wx", dx)
    own_w = pltpu.make_async_copy(wsend.at[x], wbuf.at[zl, c, x, zh], loc.at[2])
    own_w.start()
    own_w.wait()

    right, left = at(x_=xs[1]), at(x_=xs[3])

    def from_y(p):
        ref = tok.at[x, ys[(4 - p) % 4]]
        arrived(ref, "y", p)
        start(ref, ref, right, "xr", p)
        start(ref, ref, left, "xl", p)

    def from_left(p):
        ref = tok.at[xs[3], ys[(4 - p) % 4]]
        arrived(ref, "xr", p)
        if p in (0, 3):
            start(ref, ref, right, "fr", p)

    def from_right(p):
        ref = tok.at[xs[1], ys[(4 - p) % 4]]
        arrived(ref, "xl", p)
        if p in (1, 2):
            start(ref, ref, left, "fl", p)

    up_z, down_z, sibling = at(z_=zs_[1]), at(z_=zs_[7]), at(c_=1 - c)

    def blk(i, core, h):
        z_ = zs_[i % Z]
        return wbuf.at[lax.rem(z_, ZL), core, pl.ds(2 * h, 2), z_ // ZL]

    def own_block():
        for dx in range(1, 4):
            arrived(wbuf.at[zl, c, xs[4 - dx], zh], "wx", dx)
        for h in range(2):
            ref = blk(0, c, h)
            start(ref, ref, up_z, "zr", 0, h)
            start(ref, ref, down_z, "zl", 0, h)
        for h in range(2):
            ref = blk(0, c, h)
            start(ref, ref, sibling, "sr", 0, h)

    def ring(d):
        for h in range(2):
            if d < 4 or h == 0:
                ref = blk(Z - d, c, h)
                arrived(ref, "zr", d - 1, h)
                if d < 3 or (d == 3 and h == 0):
                    start(ref, ref, up_z, "zr", d, h)
                start(ref, ref, sibling, "sr", d, h)
            if d < 4 or h == 1:
                ref = blk(d, c, h)
                arrived(ref, "zl", d - 1, h)
                if d < 3 or (d == 3 and h == 1):
                    start(ref, ref, down_z, "zl", d, h)
                start(ref, ref, sibling, "sl", d, h)

    from_y(1)
    from_y(3)
    own_block()
    from_left(0)
    from_y(2)
    from_right(1)
    ring(1)
    from_left(3)
    ring(2)
    from_right(2)
    ring(3)
    ring(4)
    for d in range(5):
        for h in range(2):
            if d < 4 or h == 0:
                arrived(blk(Z - d, 1 - c, h), "sr", d, h)
            if 0 < d < 4 or (d == 4 and h == 1):
                arrived(blk(d, 1 - c, h), "sl", d, h)

    def product(b, x_):
        a = tok[x_].reshape(Y * RB, KS)
        w = wbuf[...].reshape(KS, NB)
        acc = jnp.dot(a, w, preferred_element_type=jnp.float32)
        cf[b] = acc.reshape(Y, RB, NB)
        cb[b] = acc.astype(jnp.bfloat16).reshape(Y, RB, NB)
        for dy in (1, 3, 2):
            start(cb.at[b, ys[dy]], cin.at[b, dy], at(y_=ys[dy]), "c", b, dy)

    partner = at(z_=zs_[4])

    def finish(b, x_):
        v = cf[b, y]
        for dy in (1, 3, 2):
            arrived(cin.at[b, dy], "c", b, dy)
            v = v + cin[b, dy].astype(jnp.float32)
        if b == 0:
            r = rsend[...]
        else:
            dx = (1, 3, 2)[b - 1]
            arrived(rbuf.at[dx], "r", dx)
            r = rbuf[dx]
        v = v * r[:, :1]
        cf[b, 0, :, :HC] = v[:, :HC]
        cf[b, 1, :, :HC] = v[:, HC:]
        zs[b, 0] = v[:, :HC].astype(jnp.bfloat16)
        zs[b, 1] = v[:, HC:].astype(jnp.bfloat16)
        start(zs.at[b, 1 - zh], zin.at[b], partner, "zx", b)
        out_ref[x_ * 2 + zh] = cf[b, zh, :, :HC]

    pltpu.make_async_copy(tok.at[x, y], tok.at[x, y], loc.at[1]).wait()
    order = (x, xs[3], xs[1], xs[2])
    product(0, order[0])
    for p in (1, 2):
        from_left(p)
    product(1, order[1])
    for p in (0, 3):
        from_right(p)
    product(2, order[2])
    finish(0, order[0])
    finish(1, order[1])
    for p in (0, 3):
        arrived(tok.at[xs[2], ys[(4 - p) % 4]], "fr", p)
    for p in (1, 2):
        arrived(tok.at[xs[2], ys[(4 - p) % 4]], "fl", p)
    product(3, order[3])
    finish(2, order[2])
    finish(3, order[3])
    for b in range(4):
        arrived(zin.at[b], "zx", b)
        out_ref[order[b] * 2 + 1 - zh] = zin[b].astype(jnp.float32)
    for src, dst, dev, key in sent:
        copy(src, dst, dev, *key).wait_send()


def on_device(tokens, gain, stale, bias, first, second, grad, residual, exponent):
    new_first = 0.9 * first + 0.1 * grad
    new_second = 0.95 * second + 0.05 * grad * grad
    vmem = pl.BlockSpec(memory_space=pltpu.VMEM)
    out = pl.pallas_call(
        kernel,
        out_shape=jax.ShapeDtypeStruct((8, RB, HC), jnp.float32),
        in_specs=[vmem, vmem, pl.BlockSpec(memory_space=pl.ANY)] + [vmem] * 5,
        out_specs=vmem,
        scratch_shapes=[
            pltpu.VMEM((X, Y, RB, KS), jnp.bfloat16),
            pltpu.VMEM((ZL, C, X, ZH, RB, NB), jnp.bfloat16),
            pltpu.VMEM((8, RB, HC), jnp.bfloat16),
            pltpu.VMEM((RB, 2048), jnp.float32),
            pltpu.VMEM((X, RB, NB), jnp.bfloat16),
            pltpu.VMEM((X, RB, 128), jnp.float32),
            pltpu.VMEM((RB, 128), jnp.float32),
            pltpu.VMEM((4, Y, RB, NB), jnp.float32),
            pltpu.VMEM((4, Y, RB, NB), jnp.bfloat16),
            pltpu.VMEM((4, Y, RB, NB), jnp.bfloat16),
            pltpu.VMEM((4, 2, RB, HC), jnp.bfloat16),
            pltpu.VMEM((4, RB, HC), jnp.bfloat16),
            pltpu.SemaphoreType.DMA((NIDS,)),
            pltpu.SemaphoreType.DMA((NIDS,)),
            pltpu.SemaphoreType.DMA((3,)),
        ],
        compiler_params=pltpu.CompilerParams(collective_id=0, has_side_effects=True),
    )(tokens, gain.reshape(64, 128), stale, first, second, grad, residual, exponent)
    projected = (out.reshape(256, HC) + bias[None, :]).astype(jnp.bfloat16)
    return (new_first, new_second, projected)


def solution(mesh):
    return jax.shard_map(
        on_device,
        mesh=mesh,
        in_specs=(
            P(("dp", "tensor"), None),
            P(),
            P(None, "tensor"),
            P("tensor"),
            P(("dp", "tensor"), None),
            P(("dp", "tensor"), None),
            P(("dp", "tensor"), None),
            P(("dp", "tensor"), None),
            P(("dp", "tensor"), None),
        ),
        out_specs=(P(("dp", "tensor"), None), P(("dp", "tensor"), None), P("dp", "tensor")),
        check_vma=False,
    )
```

time: 274 us -> 62 us (0.23)
  waiting for transfers between devices: 210 us -> 0 us
  Pallas kernels: 0 us -> 58.6 us
  local copies, waits for them, and re-layouts: 20.8 us -> 0.02 us
  between operations: 15.5 us -> 0.69 us
  other arithmetic: 14.1 us -> 2.5 us
  starting transfers between devices: 7.99 us -> 0 us
  matrix products: 5.37 us -> 0 us
    all_gather x2 -> x0, waiting for transfers between devices: 131 us -> none  [the longest x1 66.8 us: on_device(): gathered = lax.all_gather(delta, 'dp', axis=0, tiled=True)]
    all_to_all x1 -> x0, waiting for transfers between devices: 78.9 us -> none  [on_device(): lax.all_to_all(gathered, 'tensor', split_axis=1, concat_axis=0, tiled=True)]
    pallas_call x0 -> x1, Pallas kernels: none -> 58.6 us  [on_device(): pl.pallas_call(kernel, out_shape=jax.ShapeDtypeStruct((8, RB, HC), jnp.fl...]
    convert_element_type x2 -> x0, local copies, waits for them, and re-layouts: 13.5 us -> none  [on_device(): ordered.astype(jnp.float32)]
    convert_element_type x5 -> x1, other arithmetic: 11.1 us -> 1.63 us  [on_device(): projected = (out.reshape(256, HC) + bias[None, :]).astype(jnp.bfloat16)]
    all_to_all x1 -> x0, starting transfers between devices: 7.92 us -> none  [on_device(): lax.all_to_all(gathered, 'tensor', split_axis=1, concat_axis=0, tiled=True)]
    all_gather x1 -> x0, local copies, waits for them, and re-layouts: 6.38 us -> none  [on_device(): gathered = lax.all_gather(delta, 'dp', axis=0, tiled=True)]
    dot_general x1 -> x0, matrix products: 5.37 us -> none  [on_device(): product = jnp.dot(whole, merged, preferred_element_type=jnp.float32)]
  transfers between devices with their start and end apart: 3 -> 0, of which waited for: 3 -> 0; matrix products, arithmetic and copies ran while one was open for 9% -> 0% of each run, Pallas kernels for 0% -> 0%
where the time goes in v1:
time: 62 us; the launch traced here: 61.8 us
  Pallas kernels  58.6 us (95%)
  other arithmetic  2.5 us (4%)
  between operations  0.69 us (1%)
    pallas_call x1, Pallas kernels, on_device(): pl.pallas_call(kernel, out_shape=jax.ShapeDtypeStruct((8, RB, HC), jnp.fl...  58.6 us
    convert_element_type x1, other arithmetic, on_device(): projected = (out.reshape(256, HC) + bias[None, :]).astype(jnp.bfloat16)  1.63 us

profile of v1, /device:TPU:1, one launch (start us, length us, event | category | flops | bytes accessed | tf_op | source)
XLA Modules:
  0.0 61.8 jit_solution(6085285646155064631)
XLA Ops:
  0.6 0.0 copy-start
  0.6 0.0 copy-start.1
  0.7 0.0 copy-start.2
  0.7 0.0 copy-start.3
  0.7 58.6 %shard_map.112 = f32[8,32,256]{2,1,0:T(8,128)} custom-call(bf16[32,8192]{1,0:T(8,128)(2,1)} %tok_ref.1, f32[64,128]{1,0:T(8,128)} %bitcast.5, bf16[8192,256]{1,0:T(8,128)(2,1)} %stale_ref.1, f32[32,2048]{1,0:T(8,128)} %first_ref.1, f32[32,2048]{1,0:T(8,128)} %second_ref.1, f32[32,2048]{1,0:T(8,128)} %grad_ref.1, f32[32,2048]{1,0:T(8,128)} %resid_ref.1, ...), custom_call_target="tpu_custom_call" | custom-call | tf_op jit(solution)/shard_map/pallas_call | solution.py:306
  59.3 0.0 copy-done.3
  59.3 1.6 %fusion.1 = bf16[256,256]{1,0:T(8,128)(2,1)} fusion(f32[8,32,256]{2,1,0:T(8,128)} %shard_map.112, f32[256]{0:T(256)S(1)} %copy-done.3), kind=kLoop, calls=%fused_computation.3 | loop fusion | flops 131072 | bytes 394240 | tf_op jit(solution)/shard_map/convert_element_type | solution.py:330
  60.9 0.0 copy-done
  60.9 0.0 copy-done.1
  60.9 0.0 copy-done.2
  61.0 0.9 %fusion = (f32[32,2048]{1,0:T(8,128)}, f32[32,2048]{1,0:T(8,128)}) fusion(f32[32,2048]{1,0:T(8,128)S(1)} %copy-done, f32[32,2048]{1,0:T(8,128)S(1)} %copy-done.1, f32[32,2048]{1,0:T(8,128)S(1)} %copy-done.2), kind=kLoop, calls=%fused_computation.1 | loop fusion | flops 458752 | bytes 1310720 | tf_op jit(solution)/shard_map/add | solution.py:304
Async XLA Ops:
  0.6 60.3 %copy-start = (f32[32,2048]{1,0:T(8,128)S(1)}, f32[32,2048]{1,0:T(8,128)}, u32[]{:S(2)}) copy-start(f32[32,2048]{1,0:T(8,128)} %grad_ref.1) | copy-start | bytes 786436
  0.6 60.3 %copy-start.1 = (f32[32,2048]{1,0:T(8,128)S(1)}, f32[32,2048]{1,0:T(8,128)}, u32[]{:S(2)}) copy-start(f32[32,2048]{1,0:T(8,128)} %second_ref.1) | copy-start | bytes 786436
  0.7 60.3 %copy-start.2 = (f32[32,2048]{1,0:T(8,128)S(1)}, f32[32,2048]{1,0:T(8,128)}, u32[]{:S(2)}) copy-start(f32[32,2048]{1,0:T(8,128)} %first_ref.1) | copy-start | bytes 786436
  0.7 58.6 %copy-start.3 = (f32[256]{0:T(256)S(1)}, f32[256]{0:T(256)}, u32[]{:S(2)}) copy-start(f32[256]{0:T(256)} %param.12) | copy-start | bytes 3076

commit v2 on v0

v2 whole, which is shorter than its diff:
```python
import jax
import jax.numpy as jnp
from jax import lax
from jax.experimental import pallas as pl
from jax.experimental.pallas import tpu as pltpu
from jax.sharding import PartitionSpec as P

MESH = pl.DeviceIdType.MESH
X, Y, ZL, ZH, C = 4, 4, 4, 2, 2
Z = ZL * ZH
RB = 32
KS = 2048
HC = 256


def ids():
    table = {}

    def add(*key):
        table[key] = len(table)

    add("stale")
    for i in range(1, 4):
        add("y", i)
        add("r", i)
        add("d", i)
    for p in range(4):
        add("xr", p)
        add("xl", p)
    add("fr", 1)
    add("fl", 3)
    for p in (0, 2):
        add("fr", p)
        add("fl", p)
    for d in range(4):
        for g in range(4):
            if d < 3 or g < 2:
                add("zr", d, g)
            if d < 3 or g >= 2:
                add("zl", d, g)
    for d in range(5):
        add("sr", d)
        if d:
            add("sl", d)
    for b in range(4):
        add("zx", b)
        for dy in range(1, 4):
            add("c", b, dy)
    return table


IDS = ids()


def kernel(
    tok_in, gain_ref, stale_ref, bias_ref, first_in, second_in, grad_in, resid_in, expo_ref,
    out_ref,
    tokv, first_ref, second_ref, grad_ref, resid_ref,
    tok, wbuf, sloc, spart, dsend, drecv, rbuf, rsend, cf, cb, cin, zs, zin, send, recv, loc,
):
    dp = lax.axis_index("dp")
    t = lax.axis_index("tensor")
    c = lax.rem(dp, C)
    y = lax.rem(dp // C, Y)
    zl = dp // (C * Y)
    x = t // ZH
    zh = lax.rem(t, ZH)
    z = zh * ZL + zl

    def at(x_=None, y_=None, z_=None, c_=None):
        x_ = x if x_ is None else x_
        y_ = y if y_ is None else y_
        z_ = z if z_ is None else z_
        c_ = c if c_ is None else c_
        return ((lax.rem(z_, ZL) * Y + y_) * C + c_, x_ * ZH + z_ // ZL)

    xs = [lax.rem(x + i, X) for i in range(X)]
    ys = [lax.rem(y + i, Y) for i in range(Y)]
    zr = [lax.rem(z + i, Z) for i in range(Z)]
    right, left = at(x_=xs[1]), at(x_=xs[3])
    up_z, down_z, sibling = at(z_=zr[1]), at(z_=zr[7]), at(c_=1 - c)
    mirror, partner = at(z_=Z - 1 - z), at(z_=zr[4])

    def copy(src, dst, dev, *key):
        i = IDS[key]
        return pltpu.make_async_remote_copy(
            src_ref=src, dst_ref=dst, send_sem=send.at[i], recv_sem=recv.at[i],
            device_id=dev, device_id_type=MESH,
        )

    sent = []

    def start(src, dst, dev, *key):
        copy(src, dst, dev, *key).start()
        sent.append((dst, dev, key))

    def arrived(ref, *key):
        copy(ref, ref, right, *key).wait_recv()

    barrier = pltpu.get_barrier_semaphore()
    partners = (
        [mirror, at(x_=xs[2]), at(y_=ys[2]), up_z, down_z, right, left]
        + [at(y_=ys[1]), at(y_=ys[3]), sibling]
    )
    for dev in partners:
        pl.semaphore_signal(barrier, inc=1, device_id=dev, device_id_type=MESH)

    loads = []
    for i, (src, dst) in enumerate((
        (first_in, first_ref), (second_in, second_ref), (grad_in, grad_ref),
        (resid_in, resid_ref), (tok_in, tokv),
    )):
        loads.append(pltpu.make_async_copy(src, dst, loc.at[i]))
        loads[-1].start()

    def stale_rows(dp_, xp, zh_):
        return stale_ref.at[pl.ds(pl.multiple_of(dp_ * 256 + xp * 64 + zh_ * RB, RB), RB), :]

    for xp in range(X):
        pltpu.make_async_copy(stale_rows(dp, xp, zh), sloc.at[xp], loc.at[5]).start()

    for load in loads[:4]:
        load.wait()
    for j in range(16):
        cols = slice(j * 128, (j + 1) * 128)
        g = grad_ref[:, cols]
        nf = 0.9 * first_ref[:, cols] + 0.1 * g
        ns = 0.95 * second_ref[:, cols] + 0.05 * g * g
        corrected = 0.02 * nf / (jnp.sqrt(ns) + 1e-08) + resid_ref[:, cols]
        e = jnp.broadcast_to(expo_ref[:, j:j + 1], (RB, 128))
        up = lax.shift_left(jnp.ones_like(e), e).astype(jnp.float32)
        down = lax.shift_left(jnp.ones_like(e), 30 - e).astype(jnp.float32) * (2.0 ** -30)
        q = jnp.clip(corrected * up, -448.0, 448.0).astype(jnp.bfloat16)
        dsend[j // 4, (j // 2) % 2, :, (j % 2) * 128:(j % 2 + 1) * 128] = (
            q.astype(jnp.float32) * down
        ).astype(jnp.bfloat16)

    lane = lax.broadcasted_iota(jnp.int32, (RB, 128), 1)
    row = lax.broadcasted_iota(jnp.int32, (RB, 128), 0)
    gcol = []
    for xp in range(X):
        grow = jnp.broadcast_to(gain_ref[pl.ds(dp * 2 + xp // 2, 1), :], (RB, 128))
        hit = lane == row + (xp % 2) * 64 + zh * RB
        gcol.append(jnp.sum(jnp.where(hit, grow, 0.0), axis=1, keepdims=True))

    loads[4].wait()
    total = jnp.zeros((RB, 1), jnp.float32)
    for k in range(8):
        v = tokv[:, k * 1024:(k + 1) * 1024].astype(jnp.float32)
        total = total + jnp.sum(v * v, axis=1, keepdims=True)
    rsend[...] = jnp.broadcast_to(lax.rsqrt(total / 8192.0 + 1e-06), (RB, 128))

    pl.semaphore_wait(barrier, len(partners))

    for dx in (1, 3, 2):
        start(dsend.at[xs[dx]], drecv.at[dx], at(x_=xs[dx]), "d", dx)
    dp_m = ((ZL - 1 - zl) * Y + y) * C + c
    for xp in range(X):
        copy(stale_rows(dp_m, xp, 1 - zh), spart.at[xp], mirror, "stale").start()
    sent.append((spart, mirror, ("stale",)))

    def part(k, y_):
        return tokv.at[:, pl.ds(pl.multiple_of(k * 2048 + y_ * 512, 512), 512)]

    def spread(dev, y_, *key):
        for k in range(ZL):
            copy(part(k, y_), tok.at[x, y, :, pl.ds(k * 512, 512)], dev, *key).start()
        sent.append((tok.at[x, y], dev, key))

    spread(at(y_=ys[1]), ys[1], "y", 1)
    spread(at(y_=ys[3]), ys[3], "y", 3)
    spread(right, y, "xr", 0)
    spread(left, y, "xl", 0)
    spread(at(y_=ys[2]), ys[2], "y", 2)
    for k in range(ZL):
        pltpu.make_async_copy(part(k, y), tok.at[x, y, :, pl.ds(k * 512, 512)], loc.at[6]).start()
    for dx in range(1, 4):
        start(rsend, rbuf.at[dx], at(x_=xs[dx]), "r", dx)

    def merge(dx, half, stale):
        xp = xs[(4 - dx) % 4]
        d = dsend[xp, half] if dx == 0 else drecv[dx, half]
        g = gcol[3]
        for i in range(3):
            g = jnp.where(xp == i, gcol[i], g)
        w = g * (stale[xp].astype(jnp.float32) + d.astype(jnp.float32))
        wbuf[zl, c, xp, zh, half] = w.astype(jnp.bfloat16)

    def piece(i, g):
        z_ = zr[i % Z]
        zh_ = z_ // ZL
        half = zh_ if g < 2 else 1 - zh_
        return wbuf.at[lax.rem(z_, ZL), c, pl.ds(2 * (g % 2), 2), zh_, half]

    def whole(i, core):
        z_ = zr[i % Z]
        return wbuf.at[lax.rem(z_, ZL), core, :, z_ // ZL]

    def half_of(i, core, other):
        z_ = zr[i % Z]
        zh_ = z_ // ZL
        return wbuf.at[lax.rem(z_, ZL), core, :, zh_, 1 - zh_ if other else zh_]

    pltpu.make_async_copy(sloc, sloc, loc.at[5]).wait()
    merge(0, zh, sloc)
    for dx in (1, 3, 2):
        arrived(drecv.at[dx], "d", dx)
        merge(dx, zh, sloc)
    for g in range(2):
        start(piece(0, g), piece(0, g), up_z, "zr", 0, g)
        start(piece(0, g), piece(0, g), down_z, "zl", 0, g)
    arrived(spart, "stale")
    for dx in range(4):
        merge(dx, 1 - zh, spart)
    for g in range(2, 4):
        start(piece(0, g), piece(0, g), up_z, "zr", 0, g)
        start(piece(0, g), piece(0, g), down_z, "zl", 0, g)
    start(whole(0, c), whole(0, c), sibling, "sr", 0)

    def from_y(p):
        ref = tok.at[x, ys[(4 - p) % 4]]
        arrived(ref, "y", p)
        start(ref, ref, right, "xr", p)
        start(ref, ref, left, "xl", p)

    def token(i, p, rows=None):
        ref = tok.at[xs[i], ys[(4 - p) % 4]]
        return ref if rows is None else ref.at[pl.ds(rows, RB // 2), :]

    def ring(d):
        for g in range(4):
            if d < 4 or g < 2:
                ref = piece(Z - d, g)
                arrived(ref, "zr", d - 1, g)
                if d < 3 or (d == 3 and g < 2):
                    start(ref, ref, up_z, "zr", d, g)
            if d < 4 or g >= 2:
                ref = piece(d, g)
                arrived(ref, "zl", d - 1, g)
                if d < 3 or (d == 3 and g >= 2):
                    start(ref, ref, down_z, "zl", d, g)
        if d < 4:
            start(whole(Z - d, c), whole(Z - d, c), sibling, "sr", d)
            start(whole(d, c), whole(d, c), sibling, "sl", d)
        else:
            start(half_of(4, c, 0), half_of(4, c, 0), sibling, "sr", d)
            start(half_of(4, c, 1), half_of(4, c, 1), sibling, "sl", d)

    from_y(1)
    from_y(3)
    ring(1)
    from_y(2)
    ring(2)
    arrived(token(3, 1), "xr", 1)
    start(token(3, 1), token(3, 1), right, "fr", 1)
    arrived(token(1, 3), "xl", 3)
    start(token(1, 3), token(1, 3), left, "fl", 3)
    ring(3)
    for p in (2, 0):
        arrived(token(3, p), "xr", p)
        start(token(3, p, 0), token(3, p, 0), right, "fr", p)
        arrived(token(1, p), "xl", p)
        start(token(1, p, 16), token(1, p, 16), left, "fl", p)
    ring(4)
    for d in range(4):
        arrived(whole(Z - d, 1 - c), "sr", d)
        if d:
            arrived(whole(d, 1 - c), "sl", d)
    arrived(half_of(4, 1 - c, 0), "sr", 4)
    arrived(half_of(4, 1 - c, 1), "sl", 4)

    def weights(half):
        return wbuf[:, :, :, :, half].reshape(KS, HC)

    def send_partial(b, dy):
        start(cb.at[b, ys[dy]], cin.at[b, dy], at(y_=ys[dy]), "c", b, dy)

    def product(b, x_):
        a = tok[x_].reshape(Y * RB, KS)
        for half in range(2):
            acc = jnp.dot(a, weights(half), preferred_element_type=jnp.float32)
            acc = acc.reshape(Y, RB, HC)
            cf[b, :, half] = acc
            cb[b, :, half] = acc.astype(jnp.bfloat16)
        for dy in (1, 3, 2):
            send_partial(b, dy)

    order = (x, xs[3], xs[1], xs[2])

    def finish(b):
        if b == 0:
            r = rsend[:, :1]
        else:
            dx = (1, 3, 2)[b - 1]
            arrived(rbuf.at[dx], "r", dx)
            r = rbuf[dx, :, :1]
        for dy in (1, 3, 2):
            arrived(cin.at[b, dy], "c", b, dy)

        def total_of(half):
            v = cf[b, y, half]
            for dy in range(1, 4):
                v = v + cin[b, dy, half].astype(jnp.float32)
            return v * r

        zs[b] = total_of(1 - zh).astype(jnp.bfloat16)
        start(zs.at[b], zin.at[b], partner, "zx", b)
        out_ref[order[b] * 2 + zh] = (total_of(zh) + bias_ref[...]).astype(jnp.bfloat16)

    pltpu.make_async_copy(tok.at[x, y], tok.at[x, y], loc.at[6]).wait()
    product(0, order[0])
    arrived(token(3, 3), "xr", 3)
    product(1, order[1])
    arrived(token(1, 1), "xl", 1)
    product(2, order[2])
    arrived(token(2, 1), "fr", 1)
    arrived(token(2, 3), "fl", 3)
    arrived(token(2, 2, 0), "fr", 2)
    arrived(token(2, 2, 16), "fl", 2)
    a = jnp.concatenate([tok[xs[2], ys[dy]] for dy in (1, 2, 3)], axis=0)
    for half in range(2):
        acc = jnp.dot(a, weights(half), preferred_element_type=jnp.float32)
        for i, dy in enumerate((1, 2, 3)):
            cb[3, ys[dy], half] = acc[i * RB:(i + 1) * RB].astype(jnp.bfloat16)
    for dy in (1, 3, 2):
        send_partial(3, dy)
    for b in range(3):
        finish(b)
    arrived(token(2, 0, 0), "fr", 0)
    arrived(token(2, 0, 16), "fl", 0)
    a = tok[xs[2], y]
    for half in range(2):
        cf[3, y, half] = jnp.dot(a, weights(half), preferred_element_type=jnp.float32)
    finish(3)
    for b in range(4):
        arrived(zin.at[b], "zx", b)
        out_ref[order[b] * 2 + 1 - zh] = (
            zin[b].astype(jnp.float32) + bias_ref[...]
        ).astype(jnp.bfloat16)
    for dst, dev, key in sent:
        copy(dst, dst, dev, *key).wait_send()


def on_device(tokens, gain, stale, bias, first, second, grad, residual, exponent):
    new_first = 0.9 * first + 0.1 * grad
    new_second = 0.95 * second + 0.05 * grad * grad
    vmem = pl.BlockSpec(memory_space=pltpu.VMEM)
    there = pl.BlockSpec(memory_space=pl.ANY)
    bf16, f32 = jnp.bfloat16, jnp.float32
    out = pl.pallas_call(
        kernel,
        out_shape=jax.ShapeDtypeStruct((8, RB, HC), bf16),
        in_specs=[there, vmem, there, vmem, there, there, there, there, vmem],
        out_specs=vmem,
        scratch_shapes=[
            pltpu.VMEM((RB, 8192), bf16),
            pltpu.VMEM((RB, 2048), f32),
            pltpu.VMEM((RB, 2048), f32),
            pltpu.VMEM((RB, 2048), f32),
            pltpu.VMEM((RB, 2048), f32),
            pltpu.VMEM((X, Y, RB, KS), bf16),
            pltpu.VMEM((ZL, C, X, ZH, 2, RB, HC), bf16),
            pltpu.VMEM((X, RB, HC), bf16),
            pltpu.VMEM((X, RB, HC), bf16),
            pltpu.VMEM((X, 2, RB, HC), bf16),
            pltpu.VMEM((X, 2, RB, HC), bf16),
            pltpu.VMEM((X, RB, 128), f32),
            pltpu.VMEM((RB, 128), f32),
            pltpu.VMEM((4, Y, 2, RB, HC), f32),
            pltpu.VMEM((4, Y, 2, RB, HC), bf16),
            pltpu.VMEM((4, Y, 2, RB, HC), bf16),
            pltpu.VMEM((4, RB, HC), bf16),
            pltpu.VMEM((4, RB, HC), bf16),
            pltpu.SemaphoreType.DMA((len(IDS),)),
            pltpu.SemaphoreType.DMA((len(IDS),)),
            pltpu.SemaphoreType.DMA((7,)),
        ],
        compiler_params=pltpu.CompilerParams(collective_id=0, has_side_effects=True),
    )(
        tokens, gain.reshape(64, 128), stale, bias.reshape(1, HC),
        first, second, grad, residual, exponent,
    )
    return (new_first, new_second, out.reshape(256, HC))


def solution(mesh):
    rows = P(("dp", "tensor"), None)
    return jax.shard_map(
        on_device,
        mesh=mesh,
        in_specs=(rows, P(), P(None, "tensor"), P("tensor"), rows, rows, rows, rows, rows),
        out_specs=(rows, rows, P("dp", "tensor")),
        check_vma=False,
    )
```

time: 274 us -> 50 us (0.18)
  waiting for transfers between devices: 210 us -> 0 us
  Pallas kernels: 0 us -> 46.7 us
  local copies, waits for them, and re-layouts: 20.8 us -> 1.58 us
  between operations: 15.5 us -> 0.69 us
  other arithmetic: 14.1 us -> 0.87 us
  starting transfers between devices: 7.99 us -> 0 us
  matrix products: 5.37 us -> 0 us
    all_gather x2 -> x0, waiting for transfers between devices: 131 us -> none  [the longest x1 66.8 us: on_device(): gathered = lax.all_gather(delta, 'dp', axis=0, tiled=True)]
    all_to_all x1 -> x0, waiting for transfers between devices: 78.9 us -> none  [on_device(): lax.all_to_all(gathered, 'tensor', split_axis=1, concat_axis=0, tiled=True)]
    pallas_call x0 -> x1, Pallas kernels: none -> 46.7 us  [on_device(): pl.pallas_call(kernel, out_shape=jax.ShapeDtypeStruct((8, RB, HC), bf16),...]
    convert_element_type x2 -> x0, local copies, waits for them, and re-layouts: 13.5 us -> none  [on_device(): ordered.astype(jnp.float32)]
    convert_element_type x5 -> x0, other arithmetic: 11.1 us -> none  [the longest x1 6.46 us: on_device(): ordered.astype(jnp.float32)]
    all_to_all x1 -> x0, starting transfers between devices: 7.92 us -> none  [on_device(): lax.all_to_all(gathered, 'tensor', split_axis=1, concat_axis=0, tiled=True)]
    all_gather x1 -> x0, local copies, waits for them, and re-layouts: 6.38 us -> none  [on_device(): gathered = lax.all_gather(delta, 'dp', axis=0, tiled=True)]
    dot_general x1 -> x0, matrix products: 5.37 us -> none  [on_device(): product = jnp.dot(whole, merged, preferred_element_type=jnp.float32)]
  transfers between devices with their start and end apart: 3 -> 0, of which waited for: 3 -> 0; matrix products, arithmetic and copies ran while one was open for 9% -> 0% of each run, Pallas kernels for 0% -> 0%
where the time goes in v2:
time: 50 us; the launch traced here: 49.8 us
  Pallas kernels  46.7 us (93%)
  local copies, waits for them, and re-layouts  1.58 us (3%)
  other arithmetic  0.87 us (2%)
  between operations  0.69 us (1%)
    pallas_call x1, Pallas kernels, on_device(): pl.pallas_call(kernel, out_shape=jax.ShapeDtypeStruct((8, RB, HC), bf16),...  46.7 us
    unnamed x7, local copies, waits for them, and re-layouts  1.58 us

profile of v2, /device:TPU:1, one launch (start us, length us, event | category | flops | bytes accessed | tf_op | source)
XLA Modules:
  0.0 49.8 jit_solution(15718390918511710507)
XLA Ops:
  0.6 0.0 copy-start
  0.6 0.0 copy-start.1
  0.7 0.0 copy-start.2
  0.7 46.7 %shard_map.112 = bf16[8,32,256]{2,1,0:T(8,128)(2,1)} custom-call(bf16[32,8192]{1,0:T(8,128)(2,1)} %tok_in.1, f32[64,128]{1,0:T(8,128)} %bitcast.4, bf16[8192,256]{1,0:T(8,128)(2,1)} %stale_ref.1, f32[1,256]{1,0:T(1,128)} %bitcast.5, f32[32,2048]{1,0:T(8,128)} %first_in.1, f32[32,2048]{1,0:T(8,128)} %second_in.1, f32[32,2048]{1,0:T(8,128)} %grad_in.1, ...), custom_call_target="tpu_custom_call" | custom-call | tf_op jit(solution)/shard_map/pallas_call | solution.py:350
  47.4 0.0 copy-done
  47.4 0.0 copy-done.1
  47.4 0.0 copy-done.2
  47.4 0.9 %fusion = (f32[32,2048]{1,0:T(8,128)}, f32[32,2048]{1,0:T(8,128)}) fusion(f32[32,2048]{1,0:T(8,128)S(1)} %copy-done, f32[32,2048]{1,0:T(8,128)S(1)} %copy-done.1, f32[32,2048]{1,0:T(8,128)S(1)} %copy-done.2), kind=kLoop, calls=%fused_computation.1 | loop fusion | flops 458752 | bytes 1310720 | tf_op jit(solution)/shard_map/add | solution.py:346
  48.3 1.6 %copy.13 = bf16[256,256]{1,0:T(8,128)(2,1)} copy(bf16[256,256]{1,0:T(8,128)(2,1)} %bitcast.3) | data formatting | bytes 262144
Async XLA Ops:
  0.6 46.7 %copy-start = (f32[32,2048]{1,0:T(8,128)S(1)}, f32[32,2048]{1,0:T(8,128)}, u32[]{:S(2)}) copy-start(f32[32,2048]{1,0:T(8,128)} %grad_in.1) | copy-start | bytes 786436
  0.6 46.7 %copy-start.1 = (f32[32,2048]{1,0:T(8,128)S(1)}, f32[32,2048]{1,0:T(8,128)}, u32[]{:S(2)}) copy-start(f32[32,2048]{1,0:T(8,128)} %second_in.1) | copy-start | bytes 786436
  0.7 46.7 %copy-start.2 = (f32[32,2048]{1,0:T(8,128)S(1)}, f32[32,2048]{1,0:T(8,128)}, u32[]{:S(2)}) copy-start(f32[32,2048]{1,0:T(8,128)} %first_in.1) | copy-start | bytes 786436

commit v3 on v2

--- a/solution.py
+++ b/solution.py
@@ -32,20 +32,18 @@
     for p in (0, 2):
         add("fr", p)
         add("fl", p)
-    for d in range(4):
-        for g in range(4):
-            if d < 3 or g < 2:
-                add("zr", d, g)
-            if d < 3 or g >= 2:
-                add("zl", d, g)
-    for d in range(5):
-        add("sr", d)
-        if d:
-            add("sl", d)
+    for h in range(2):
+        for d in range(4):
+            for cc in range(2 if d < 3 else 1):
+                add("z", h, d, cc)
+        for d in range(5):
+            for cc in range(2 if 0 < d < 4 else 1):
+                add("s", h, d, cc)
     for b in range(4):
         add("zx", b)
         for dy in range(1, 4):
-            add("c", b, dy)
+            for h in range(2):
+                add("c", b, h, dy)
     return table
 
 
@@ -80,6 +78,8 @@
     right, left = at(x_=xs[1]), at(x_=xs[3])
     up_z, down_z, sibling = at(z_=zr[1]), at(z_=zr[7]), at(c_=1 - c)
     mirror, partner = at(z_=Z - 1 - z), at(z_=zr[4])
+
+    halves = (1 - zh, zh)
 
     def copy(src, dst, dev, *key):
         i = IDS[key]
@@ -186,36 +186,35 @@
         w = g * (stale[xp].astype(jnp.float32) + d.astype(jnp.float32))
         wbuf[zl, c, xp, zh, half] = w.astype(jnp.bfloat16)
 
-    def piece(i, g):
-        z_ = zr[i % Z]
-        zh_ = z_ // ZL
-        half = zh_ if g < 2 else 1 - zh_
-        return wbuf.at[lax.rem(z_, ZL), c, pl.ds(2 * (g % 2), 2), zh_, half]
-
-    def whole(i, core):
-        z_ = zr[i % Z]
-        return wbuf.at[lax.rem(z_, ZL), core, :, z_ // ZL]
-
-    def half_of(i, core, other):
-        z_ = zr[i % Z]
-        zh_ = z_ // ZL
-        return wbuf.at[lax.rem(z_, ZL), core, :, zh_, 1 - zh_ if other else zh_]
+    way = 1 - 2 * c
+    onward = at(z_=lax.rem(z + way + Z, Z))
+
+    def block(hops, core, h):
+        z_ = lax.rem(z + way * hops + 2 * Z, Z)
+        return wbuf.at[lax.rem(z_, ZL), core, :, z_ // ZL, h]
+
+    def first_hop(h):
+        ref = block(0, c, h)
+        start(ref, ref, sibling, "s", h, 0, 0)
+        start(ref, ref, onward, "z", h, 0, 0)
+
+    def first_hop_sibling(h):
+        ref = block(0, 1 - c, h)
+        arrived(ref, "s", h, 0, 0)
+        start(ref, ref, onward, "z", h, 0, 1)
 
     pltpu.make_async_copy(sloc, sloc, loc.at[5]).wait()
     merge(0, zh, sloc)
     for dx in (1, 3, 2):
         arrived(drecv.at[dx], "d", dx)
         merge(dx, zh, sloc)
-    for g in range(2):
-        start(piece(0, g), piece(0, g), up_z, "zr", 0, g)
-        start(piece(0, g), piece(0, g), down_z, "zl", 0, g)
     arrived(spart, "stale")
-    for dx in range(4):
+    for dx in (0, 1, 3, 2):
         merge(dx, 1 - zh, spart)
-    for g in range(2, 4):
-        start(piece(0, g), piece(0, g), up_z, "zr", 0, g)
-        start(piece(0, g), piece(0, g), down_z, "zl", 0, g)
-    start(whole(0, c), whole(0, c), sibling, "sr", 0)
+    first_hop(0)
+    first_hop(1)
+    first_hop_sibling(0)
+    first_hop_sibling(1)
 
     def from_y(p):
         ref = tok.at[x, ys[(4 - p) % 4]]
@@ -228,110 +227,124 @@
         return ref if rows is None else ref.at[pl.ds(rows, RB // 2), :]
 
     def ring(d):
-        for g in range(4):
-            if d < 4 or g < 2:
-                ref = piece(Z - d, g)
-                arrived(ref, "zr", d - 1, g)
-                if d < 3 or (d == 3 and g < 2):
-                    start(ref, ref, up_z, "zr", d, g)
-            if d < 4 or g >= 2:
-                ref = piece(d, g)
-                arrived(ref, "zl", d - 1, g)
-                if d < 3 or (d == 3 and g >= 2):
-                    start(ref, ref, down_z, "zl", d, g)
-        if d < 4:
-            start(whole(Z - d, c), whole(Z - d, c), sibling, "sr", d)
-            start(whole(d, c), whole(d, c), sibling, "sl", d)
+        for cc in range(2 if d < 4 else 1):
+            for h in range(2):
+                ref = block(-d, 1 - c if cc else c, h)
+                arrived(ref, "z", h, d - 1, cc)
+                if d < 3 or (d == 3 and cc == 0):
+                    start(ref, ref, onward, "z", h, d, cc)
+                start(ref, ref, sibling, "s", h, d, cc)
+
+    def forward(p):
+        if p == 1:
+            arrived(token(3, 1), "xr", 1)
+            start(token(3, 1), token(3, 1), right, "fr", 1)
+            arrived(token(1, 3), "xl", 3)
+            start(token(1, 3), token(1, 3), left, "fl", 3)
         else:
-            start(half_of(4, c, 0), half_of(4, c, 0), sibling, "sr", d)
-            start(half_of(4, c, 1), half_of(4, c, 1), sibling, "sl", d)
+            arrived(token(3, p), "xr", p)
+            start(token(3, p, 0), token(3, p, 0), right, "fr", p)
+            arrived(token(1, p), "xl", p)
+            start(token(1, p, 16), token(1, p, 16), left, "fl", p)
+
+    def siblings(d):
+        for cc in range(2 if d < 4 else 1):
+            for h in range(2):
+                arrived(block(d, c if cc else 1 - c, h), "s", h, d, cc)
+
+    def weights(k):
+        return wbuf[:, :, :, :, halves[k]].reshape(KS, HC)
+
+    def send_partial(b, h):
+        for dy in (1, 3, 2):
+            start(cb.at[b, h, ys[dy]], cin.at[b, h, dy], at(y_=ys[dy]), "c", b, h, dy)
+
+    def product(b, h):
+        a = tok[order[b]].reshape(Y * RB, KS)
+        acc = jnp.dot(a, weights(h), preferred_element_type=jnp.float32)
+        acc = acc.reshape(Y, RB, HC)
+        cf[b, h] = acc
+        cb[b, h] = acc.astype(jnp.bfloat16)
+        send_partial(b, h)
+
+    def product_far(h):
+        a = jnp.concatenate([tok[xs[2], ys[dy]] for dy in (1, 2, 3)], axis=0)
+        acc = jnp.dot(a, weights(h), preferred_element_type=jnp.float32)
+        for i, dy in enumerate((1, 2, 3)):
+            cb[3, h, ys[dy]] = acc[i * RB:(i + 1) * RB].astype(jnp.bfloat16)
+        send_partial(3, h)
+
+    def product_last(k):
+        cf[3, k, y] = jnp.dot(tok[xs[2], y], weights(k), preferred_element_type=jnp.float32)
+
+    order = (x, xs[3], xs[1], xs[2])
+
+    def total_of(b, k):
+        for dy in (1, 3, 2):
+            arrived(cin.at[b, k, dy], "c", b, k, dy)
+        v = cf[b, k, y]
+        for dy in range(1, 4):
+            v = v + cin[b, k, dy].astype(jnp.float32)
+        dx = (0, 1, 3, 2)[b]
+        return v * (rbuf[dx, :, :1] if b else rsend[:, :1])
+
+    def finish(b, k):
+        if k == 0:
+            if b:
+                dx = (0, 1, 3, 2)[b]
+                arrived(rbuf.at[dx], "r", dx)
+            zs[b] = total_of(b, 0).astype(jnp.bfloat16)
+            start(zs.at[b], zin.at[b], partner, "zx", b)
+        else:
+            out_ref[order[b] * 2 + zh] = (total_of(b, 1) + bias_ref[...]).astype(jnp.bfloat16)
+
+    def own_tokens():
+        pltpu.make_async_copy(tok.at[x, y], tok.at[x, y], loc.at[6]).wait()
+
+    def near_tokens():
+        arrived(token(3, 3), "xr", 3)
+        arrived(token(1, 1), "xl", 1)
+
+    def far_tokens():
+        arrived(token(2, 1), "fr", 1)
+        arrived(token(2, 3), "fl", 3)
+        arrived(token(2, 2, 0), "fr", 2)
+        arrived(token(2, 2, 16), "fl", 2)
+
+    def last_tokens():
+        arrived(token(2, 0, 0), "fr", 0)
+        arrived(token(2, 0, 16), "fl", 0)
 
     from_y(1)
     from_y(3)
     ring(1)
     from_y(2)
     ring(2)
-    arrived(token(3, 1), "xr", 1)
-    start(token(3, 1), token(3, 1), right, "fr", 1)
-    arrived(token(1, 3), "xl", 3)
-    start(token(1, 3), token(1, 3), left, "fl", 3)
+    forward(1)
     ring(3)
-    for p in (2, 0):
-        arrived(token(3, p), "xr", p)
-        start(token(3, p, 0), token(3, p, 0), right, "fr", p)
-        arrived(token(1, p), "xl", p)
-        start(token(1, p, 16), token(1, p, 16), left, "fl", p)
+    forward(2)
+    forward(0)
     ring(4)
-    for d in range(4):
-        arrived(whole(Z - d, 1 - c), "sr", d)
-        if d:
-            arrived(whole(d, 1 - c), "sl", d)
-    arrived(half_of(4, 1 - c, 0), "sr", 4)
-    arrived(half_of(4, 1 - c, 1), "sl", 4)
-
-    def weights(half):
-        return wbuf[:, :, :, :, half].reshape(KS, HC)
-
-    def send_partial(b, dy):
-        start(cb.at[b, ys[dy]], cin.at[b, dy], at(y_=ys[dy]), "c", b, dy)
-
-    def product(b, x_):
-        a = tok[x_].reshape(Y * RB, KS)
-        for half in range(2):
-            acc = jnp.dot(a, weights(half), preferred_element_type=jnp.float32)
-            acc = acc.reshape(Y, RB, HC)
-            cf[b, :, half] = acc
-            cb[b, :, half] = acc.astype(jnp.bfloat16)
-        for dy in (1, 3, 2):
-            send_partial(b, dy)
-
-    order = (x, xs[3], xs[1], xs[2])
-
-    def finish(b):
-        if b == 0:
-            r = rsend[:, :1]
-        else:
-            dx = (1, 3, 2)[b - 1]
-            arrived(rbuf.at[dx], "r", dx)
-            r = rbuf[dx, :, :1]
-        for dy in (1, 3, 2):
-            arrived(cin.at[b, dy], "c", b, dy)
-
-        def total_of(half):
-            v = cf[b, y, half]
-            for dy in range(1, 4):
-                v = v + cin[b, dy, half].astype(jnp.float32)
-            return v * r
-
-        zs[b] = total_of(1 - zh).astype(jnp.bfloat16)
-        start(zs.at[b], zin.at[b], partner, "zx", b)
-        out_ref[order[b] * 2 + zh] = (total_of(zh) + bias_ref[...]).astype(jnp.bfloat16)
-
-    pltpu.make_async_copy(tok.at[x, y], tok.at[x, y], loc.at[6]).wait()
-    product(0, order[0])
-    arrived(token(3, 3), "xr", 3)
-    product(1, order[1])
-    arrived(token(1, 1), "xl", 1)
-    product(2, order[2])
-    arrived(token(2, 1), "fr", 1)
-    arrived(token(2, 3), "fl", 3)
-    arrived(token(2, 2, 0), "fr", 2)
-    arrived(token(2, 2, 16), "fl", 2)
-    a = jnp.concatenate([tok[xs[2], ys[dy]] for dy in (1, 2, 3)], axis=0)
-    for half in range(2):
-        acc = jnp.dot(a, weights(half), preferred_element_type=jnp.float32)
-        for i, dy in enumerate((1, 2, 3)):
-            cb[3, ys[dy], half] = acc[i * RB:(i + 1) * RB].astype(jnp.bfloat16)
-    for dy in (1, 3, 2):
-        send_partial(3, dy)
+    own_tokens()
+    for d in range(1, 5):
+        siblings(d)
+    product(0, 0)
+    near_tokens()
+    product(1, 0)
+    product(2, 0)
+    far_tokens()
+    product_far(0)
     for b in range(3):
-        finish(b)
-    arrived(token(2, 0, 0), "fr", 0)
-    arrived(token(2, 0, 16), "fl", 0)
-    a = tok[xs[2], y]
-    for half in range(2):
-        cf[3, y, half] = jnp.dot(a, weights(half), preferred_element_type=jnp.float32)
-    finish(3)
+        product(b, 1)
+    product_far(1)
+    for b in range(3):
+        finish(b, 0)
+    last_tokens()
+    product_last(0)
+    finish(3, 0)
+    product_last(1)
+    for b in range(4):
+        finish(b, 1)
     for b in range(4):
         arrived(zin.at[b], "zx", b)
         out_ref[order[b] * 2 + 1 - zh] = (
@@ -366,9 +379,9 @@
             pltpu.VMEM((X, 2, RB, HC), bf16),
             pltpu.VMEM((X, RB, 128), f32),
             pltpu.VMEM((RB, 128), f32),
-            pltpu.VMEM((4, Y, 2, RB, HC), f32),
-            pltpu.VMEM((4, Y, 2, RB, HC), bf16),
-            pltpu.VMEM((4, Y, 2, RB, HC), bf16),
+            pltpu.VMEM((4, 2, Y, RB, HC), f32),
+            pltpu.VMEM((4, 2, Y, RB, HC), bf16),
+            pltpu.VMEM((4, 2, Y, RB, HC), bf16),
             pltpu.VMEM((4, RB, HC), bf16),
             pltpu.VMEM((4, RB, HC), bf16),
             pltpu.SemaphoreType.DMA((len(IDS),)),

time: 50 us -> 46 us (0.920)
  Pallas kernels: 46.7 us -> 42.7 us
    pallas_call x1, Pallas kernels: 46.7 us -> 42.7 us  [on_device(): pl.pallas_call(kernel, out_shape=jax.ShapeDtypeStruct((8, RB, HC), bf16),...]
where the time goes in v3:
time: 46 us; the launch traced here: 45.9 us
  Pallas kernels  42.7 us (93%)
  local copies, waits for them, and re-layouts  1.58 us (3%)
  other arithmetic  0.87 us (2%)
  between operations  0.69 us (2%)
    pallas_call x1, Pallas kernels, on_device(): pl.pallas_call(kernel, out_shape=jax.ShapeDtypeStruct((8, RB, HC), bf16),...  42.7 us
    unnamed x7, local copies, waits for them, and re-layouts  1.58 us

profile of v3, /device:TPU:1, one launch (start us, length us, event | category | flops | bytes accessed | tf_op | source)
XLA Modules:
  0.0 45.9 jit_solution(1621381681301218582)
XLA Ops:
  0.6 0.0 copy-start
  0.6 0.0 copy-start.1
  0.7 0.0 copy-start.2
  0.7 42.7 %shard_map.112 = bf16[8,32,256]{2,1,0:T(8,128)(2,1)} custom-call(bf16[32,8192]{1,0:T(8,128)(2,1)} %tok_in.1, f32[64,128]{1,0:T(8,128)} %bitcast.4, bf16[8192,256]{1,0:T(8,128)(2,1)} %stale_ref.1, f32[1,256]{1,0:T(1,128)} %bitcast.5, f32[32,2048]{1,0:T(8,128)} %first_in.1, f32[32,2048]{1,0:T(8,128)} %second_in.1, f32[32,2048]{1,0:T(8,128)} %grad_in.1, ...), custom_call_target="tpu_custom_call" | custom-call | tf_op jit(solution)/shard_map/pallas_call | solution.py:363
  43.4 0.0 copy-done
  43.4 0.0 copy-done.1
  43.4 0.0 copy-done.2
  43.4 0.9 %fusion = (f32[32,2048]{1,0:T(8,128)}, f32[32,2048]{1,0:T(8,128)}) fusion(f32[32,2048]{1,0:T(8,128)S(1)} %copy-done, f32[32,2048]{1,0:T(8,128)S(1)} %copy-done.1, f32[32,2048]{1,0:T(8,128)S(1)} %copy-done.2), kind=kLoop, calls=%fused_computation.1 | loop fusion | flops 458752 | bytes 1310720 | tf_op jit(solution)/shard_map/add | solution.py:359
  44.3 1.6 %copy.13 = bf16[256,256]{1,0:T(8,128)(2,1)} copy(bf16[256,256]{1,0:T(8,128)(2,1)} %bitcast.3) | data formatting | bytes 262144
Async XLA Ops:
  0.6 42.8 %copy-start = (f32[32,2048]{1,0:T(8,128)S(1)}, f32[32,2048]{1,0:T(8,128)}, u32[]{:S(2)}) copy-start(f32[32,2048]{1,0:T(8,128)} %grad_in.1) | copy-start | bytes 786436
  0.6 42.8 %copy-start.1 = (f32[32,2048]{1,0:T(8,128)S(1)}, f32[32,2048]{1,0:T(8,128)}, u32[]{:S(2)}) copy-start(f32[32,2048]{1,0:T(8,128)} %second_in.1) | copy-start | bytes 786436
  0.7 42.8 %copy-start.2 = (f32[32,2048]{1,0:T(8,128)S(1)}, f32[32,2048]{1,0:T(8,128)}, u32[]{:S(2)}) copy-start(f32[32,2048]{1,0:T(8,128)} %first_in.1) | copy-start | bytes 786436

commit v4 on v3

--- a/solution.py
+++ b/solution.py
@@ -362,7 +362,7 @@
     bf16, f32 = jnp.bfloat16, jnp.float32
     out = pl.pallas_call(
         kernel,
-        out_shape=jax.ShapeDtypeStruct((8, RB, HC), bf16),
+        out_shape=pltpu.VMEM((8, RB, HC), bf16),
         in_specs=[there, vmem, there, vmem, there, there, there, there, vmem],
         out_specs=vmem,
         scratch_shapes=[

time: 46 us -> 44.4 us (0.965)
  local copies, waits for them, and re-layouts: 1.58 us -> 0.67 us
  Pallas kernels: 42.7 us -> 42.1 us
    unnamed x7, local copies, waits for them, and re-layouts: 1.58 us -> 0.67 us
    pallas_call x1, Pallas kernels: 42.7 us -> 42.1 us  [on_device(): pl.pallas_call(kernel, out_shape=pltpu.VMEM((8, RB, HC), bf16), in_specs=...]
where the time goes in v4:
time: 44.4 us; the launch traced here: 44.3 us
  Pallas kernels  42.1 us (95%)
  other arithmetic  0.87 us (2%)
  local copies, waits for them, and re-layouts  0.67 us (2%)
  between operations  0.67 us (2%)
    pallas_call x1, Pallas kernels, on_device(): pl.pallas_call(kernel, out_shape=pltpu.VMEM((8, RB, HC), bf16), in_specs=...  42.1 us

profile of v4, /device:TPU:1, one launch (start us, length us, event | category | flops | bytes accessed | tf_op | source)
XLA Modules:
  0.0 44.3 jit_solution(14172850225250685175)
XLA Ops:
  0.6 0.0 copy-start
  0.6 0.0 copy-start.1
  0.7 0.0 copy-start.2
  0.7 42.1 %shard_map.112 = bf16[8,32,256]{2,1,0:T(8,128)(2,1)S(1)} custom-call(bf16[32,8192]{1,0:T(8,128)(2,1)} %tok_in.1, f32[64,128]{1,0:T(8,128)} %bitcast.4, bf16[8192,256]{1,0:T(8,128)(2,1)} %stale_ref.1, f32[1,256]{1,0:T(1,128)} %bitcast.5, f32[32,2048]{1,0:T(8,128)} %first_in.1, f32[32,2048]{1,0:T(8,128)} %second_in.1, f32[32,2048]{1,0:T(8,128)} %grad_in.1, ...), custom_call_target="tpu_custom_call" | custom-call | tf_op jit(solution)/shard_map/pallas_call | solution.py:363
  42.8 0.7 %copy.13 = bf16[256,256]{1,0:T(8,128)(2,1)} copy(bf16[256,256]{1,0:T(8,128)(2,1)S(1)} %bitcast.3) | data formatting | bytes 262144
  43.4 0.0 copy-done
  43.4 0.0 copy-done.1
  43.4 0.0 copy-done.2
  43.4 0.9 %fusion = (f32[32,2048]{1,0:T(8,128)}, f32[32,2048]{1,0:T(8,128)}) fusion(f32[32,2048]{1,0:T(8,128)S(1)} %copy-done, f32[32,2048]{1,0:T(8,128)S(1)} %copy-done.1, f32[32,2048]{1,0:T(8,128)S(1)} %copy-done.2), kind=kLoop, calls=%fused_computation.1 | loop fusion | flops 458752 | bytes 1310720 | tf_op jit(solution)/shard_map/add | solution.py:359
Async XLA Ops:
  0.6 42.8 %copy-start = (f32[32,2048]{1,0:T(8,128)S(1)}, f32[32,2048]{1,0:T(8,128)}, u32[]{:S(2)}) copy-start(f32[32,2048]{1,0:T(8,128)} %grad_in.1) | copy-start | bytes 786436
  0.6 42.8 %copy-start.1 = (f32[32,2048]{1,0:T(8,128)S(1)}, f32[32,2048]{1,0:T(8,128)}, u32[]{:S(2)}) copy-start(f32[32,2048]{1,0:T(8,128)} %second_in.1) | copy-start | bytes 786436
  0.7 42.8 %copy-start.2 = (f32[32,2048]{1,0:T(8,128)S(1)}, f32[32,2048]{1,0:T(8,128)}, u32[]{:S(2)}) copy-start(f32[32,2048]{1,0:T(8,128)} %first_in.1) | copy-start | bytes 786436

commit v5 on v4

--- a/solution.py
+++ b/solution.py
@@ -148,7 +148,10 @@
     for k in range(8):
         v = tokv[:, k * 1024:(k + 1) * 1024].astype(jnp.float32)
         total = total + jnp.sum(v * v, axis=1, keepdims=True)
-    rsend[...] = jnp.broadcast_to(lax.rsqrt(total / 8192.0 + 1e-06), (RB, 128))
+    scale = lax.rsqrt(total / 8192.0 + 1e-06)
+    rsend[...] = jnp.broadcast_to(
+        jnp.sum(jnp.where(lane == row, scale, 0.0), axis=0, keepdims=True), (8, 128)
+    )
 
     pl.semaphore_wait(barrier, len(partners))
 
@@ -191,7 +194,8 @@
 
     def block(hops, core, h):
         z_ = lax.rem(z + way * hops + 2 * Z, Z)
-        return wbuf.at[lax.rem(z_, ZL), core, :, z_ // ZL, h]
+        zh_ = z_ // ZL
+        return wbuf.at[lax.rem(z_, ZL), core, :, zh_, 1 - zh_ if h else zh_]
 
     def first_hop(h):
         ref = block(0, c, h)
@@ -208,13 +212,11 @@
     for dx in (1, 3, 2):
         arrived(drecv.at[dx], "d", dx)
         merge(dx, zh, sloc)
+    first_hop(0)
     arrived(spart, "stale")
     for dx in (0, 1, 3, 2):
         merge(dx, 1 - zh, spart)
-    first_hop(0)
     first_hop(1)
-    first_hop_sibling(0)
-    first_hop_sibling(1)
 
     def from_y(p):
         ref = tok.at[x, ys[(4 - p) % 4]]
@@ -226,9 +228,9 @@
         ref = tok.at[xs[i], ys[(4 - p) % 4]]
         return ref if rows is None else ref.at[pl.ds(rows, RB // 2), :]
 
-    def ring(d):
+    def ring(d, hs=(0, 1)):
         for cc in range(2 if d < 4 else 1):
-            for h in range(2):
+            for h in hs:
                 ref = block(-d, 1 - c if cc else c, h)
                 arrived(ref, "z", h, d - 1, cc)
                 if d < 3 or (d == 3 and cc == 0):
@@ -247,35 +249,53 @@
             arrived(token(1, p), "xl", p)
             start(token(1, p, 16), token(1, p, 16), left, "fl", p)
 
-    def siblings(d):
+    def siblings(d, hs=(0, 1)):
         for cc in range(2 if d < 4 else 1):
-            for h in range(2):
+            for h in hs:
                 arrived(block(d, c if cc else 1 - c, h), "s", h, d, cc)
 
-    def weights(k):
-        return wbuf[:, :, :, :, halves[k]].reshape(KS, HC)
+    def quarter(i, k):
+        return wbuf[zls[i], :, :, :, halves[k]].reshape(KS // ZL, HC)
+
+    zls = [lax.rem(zl + i, ZL) for i in range(ZL)]
+
+    def columns(i):
+        return pl.ds(pl.multiple_of(zls[i] * 512, 512), 512)
+
+    def partial(a_of, ks, k):
+        acc = None
+        for i in ks:
+            one = jnp.dot(a_of(i), quarter(i, k), preferred_element_type=jnp.float32)
+            acc = one if acc is None else acc + one
+        return acc
 
     def send_partial(b, h):
         for dy in (1, 3, 2):
             start(cb.at[b, h, ys[dy]], cin.at[b, h, dy], at(y_=ys[dy]), "c", b, h, dy)
 
-    def product(b, h):
-        a = tok[order[b]].reshape(Y * RB, KS)
-        acc = jnp.dot(a, weights(h), preferred_element_type=jnp.float32)
-        acc = acc.reshape(Y, RB, HC)
-        cf[b, h] = acc
-        cb[b, h] = acc.astype(jnp.bfloat16)
-        send_partial(b, h)
-
-    def product_far(h):
-        a = jnp.concatenate([tok[xs[2], ys[dy]] for dy in (1, 2, 3)], axis=0)
-        acc = jnp.dot(a, weights(h), preferred_element_type=jnp.float32)
+    def rows_of_block(b):
+        return lambda i: tok[order[b], :, :, columns(i)].reshape(Y * RB, KS // ZL)
+
+    def early(b, k):
+        cf[b, k] = partial(rows_of_block(b), (1, 2, 3), k).reshape(Y, RB, HC)
+
+    def product(b, k):
+        acc = cf[b, k] + partial(rows_of_block(b), (0,), k).reshape(Y, RB, HC)
+        cf[b, k] = acc
+        cb[b, k] = acc.astype(jnp.bfloat16)
+        send_partial(b, k)
+
+    def product_far(k):
+        def a_of(i):
+            return jnp.concatenate([tok[xs[2], ys[dy], :, columns(i)] for dy in (1, 2, 3)], axis=0)
+
+        acc = partial(a_of, range(ZL), k)
         for i, dy in enumerate((1, 2, 3)):
-            cb[3, h, ys[dy]] = acc[i * RB:(i + 1) * RB].astype(jnp.bfloat16)
-        send_partial(3, h)
+            cb[3, k, ys[dy]] = acc[i * RB:(i + 1) * RB].astype(jnp.bfloat16)
+        send_partial(3, k)
 
     def product_last(k):
-        cf[3, k, y] = jnp.dot(tok[xs[2], y], weights(k), preferred_element_type=jnp.float32)
+        cf[3, k, y] = partial(lambda i: tok[xs[2], y, :, columns(i)], range(ZL), k)
 
     order = (x, xs[3], xs[1], xs[2])
 
@@ -286,7 +306,9 @@
         for dy in range(1, 4):
             v = v + cin[b, k, dy].astype(jnp.float32)
         dx = (0, 1, 3, 2)[b]
-        return v * (rbuf[dx, :, :1] if b else rsend[:, :1])
+        line = rbuf[dx, :1] if b else rsend[:1]
+        line = jnp.broadcast_to(line, (RB, 128))
+        return v * jnp.sum(jnp.where(lane == row, line, 0.0), axis=1, keepdims=True)
 
     def finish(b, k):
         if k == 0:
@@ -317,6 +339,8 @@
 
     from_y(1)
     from_y(3)
+    first_hop_sibling(0)
+    first_hop_sibling(1)
     ring(1)
     from_y(2)
     ring(2)
@@ -324,16 +348,24 @@
     ring(3)
     forward(2)
     forward(0)
-    ring(4)
+    ring(4, (0,))
     own_tokens()
-    for d in range(1, 5):
+    for d in range(1, 4):
         siblings(d)
+    ring(4, (1,))
+    early(0, 0)
+    near_tokens()
+    early(1, 0)
+    early(2, 0)
+    siblings(4, (0,))
     product(0, 0)
-    near_tokens()
     product(1, 0)
     product(2, 0)
+    for b in range(3):
+        early(b, 1)
     far_tokens()
     product_far(0)
+    siblings(4, (1,))
     for b in range(3):
         product(b, 1)
     product_far(1)
@@ -377,8 +409,8 @@
             pltpu.VMEM((X, RB, HC), bf16),
             pltpu.VMEM((X, 2, RB, HC), bf16),
             pltpu.VMEM((X, 2, RB, HC), bf16),
-            pltpu.VMEM((X, RB, 128), f32),
-            pltpu.VMEM((RB, 128), f32),
+            pltpu.VMEM((X, 8, 128), f32),
+            pltpu.VMEM((8, 128), f32),
             pltpu.VMEM((4, 2, Y, RB, HC), f32),
             pltpu.VMEM((4, 2, Y, RB, HC), bf16),
             pltpu.VMEM((4, 2, Y, RB, HC), bf16),

time: 44.4 us -> 44.3 us (level); the launches traced: 44.3 us -> 43.5 us
  Pallas kernels: 42.1 us -> 41.3 us
    pallas_call x1, Pallas kernels: 42.1 us -> 41.3 us  [on_device(): pl.pallas_call(kernel, out_shape=pltpu.VMEM((8, RB, HC), bf16), in_specs=...]
where the time goes in v5:
time: 44.3 us; the launch traced here: 43.5 us
  Pallas kernels  41.3 us (93%)
  other arithmetic  0.87 us (2%)
  local copies, waits for them, and re-layouts  0.67 us (2%)
  between operations  0.67 us (2%)
    pallas_call x1, Pallas kernels, on_device(): pl.pallas_call(kernel, out_shape=pltpu.VMEM((8, RB, HC), bf16), in_specs=...  41.3 us

profile of v5, /device:TPU:1, one launch (start us, length us, event | category | flops | bytes accessed | tf_op | source)
XLA Modules:
  0.0 43.5 jit_solution(6631382127820025192)
XLA Ops:
  0.6 0.0 copy-start
  0.6 0.0 copy-start.1
  0.7 0.0 copy-start.2
  0.7 41.3 %shard_map.112 = bf16[8,32,256]{2,1,0:T(8,128)(2,1)S(1)} custom-call(bf16[32,8192]{1,0:T(8,128)(2,1)} %tok_in.1, f32[64,128]{1,0:T(8,128)} %bitcast.4, bf16[8192,256]{1,0:T(8,128)(2,1)} %stale_ref.1, f32[1,256]{1,0:T(1,128)} %bitcast.5, f32[32,2048]{1,0:T(8,128)} %first_in.1, f32[32,2048]{1,0:T(8,128)} %second_in.1, f32[32,2048]{1,0:T(8,128)} %grad_in.1, ...), custom_call_target="tpu_custom_call" | custom-call | tf_op jit(solution)/shard_map/pallas_call | solution.py:395
  42.0 0.7 %copy.13 = bf16[256,256]{1,0:T(8,128)(2,1)} copy(bf16[256,256]{1,0:T(8,128)(2,1)S(1)} %bitcast.3) | data formatting | bytes 262144
  42.7 0.0 copy-done
  42.7 0.0 copy-done.1
  42.7 0.0 copy-done.2
  42.7 0.9 %fusion = (f32[32,2048]{1,0:T(8,128)}, f32[32,2048]{1,0:T(8,128)}) fusion(f32[32,2048]{1,0:T(8,128)S(1)} %copy-done, f32[32,2048]{1,0:T(8,128)S(1)} %copy-done.1, f32[32,2048]{1,0:T(8,128)S(1)} %copy-done.2), kind=kLoop, calls=%fused_computation.1 | loop fusion | flops 458752 | bytes 1310720 | tf_op jit(solution)/shard_map/add | solution.py:391
Async XLA Ops:
  0.6 42.0 %copy-start = (f32[32,2048]{1,0:T(8,128)S(1)}, f32[32,2048]{1,0:T(8,128)}, u32[]{:S(2)}) copy-start(f32[32,2048]{1,0:T(8,128)} %grad_in.1) | copy-start | bytes 786436
  0.6 42.0 %copy-start.1 = (f32[32,2048]{1,0:T(8,128)S(1)}, f32[32,2048]{1,0:T(8,128)}, u32[]{:S(2)}) copy-start(f32[32,2048]{1,0:T(8,128)} %second_in.1) | copy-start | bytes 786436
  0.7 42.0 %copy-start.2 = (f32[32,2048]{1,0:T(8,128)S(1)}, f32[32,2048]{1,0:T(8,128)}, u32[]{:S(2)}) copy-start(f32[32,2048]{1,0:T(8,128)} %first_in.1) | copy-start | bytes 786436

commit v6 on v5

--- a/solution.py
+++ b/solution.py
@@ -21,12 +21,14 @@
 
     add("stale")
     for i in range(1, 4):
-        add("y", i)
         add("r", i)
         add("d", i)
     for p in range(4):
-        add("xr", p)
-        add("xl", p)
+        for half in range(2 if p in (1, 3) else 1):
+            if p:
+                add("y", p, half)
+            add("xr", p, half)
+            add("xl", p, half)
     add("fr", 1)
     add("fl", 3)
     for p in (0, 2):
@@ -34,10 +36,10 @@
         add("fl", p)
     for h in range(2):
         for d in range(4):
-            for cc in range(2 if d < 3 else 1):
+            for cc in range(2):
                 add("z", h, d, cc)
         for d in range(5):
-            for cc in range(2 if 0 < d < 4 else 1):
+            for cc in range(2 if d else 1):
                 add("s", h, d, cc)
     for b in range(4):
         add("zx", b)
@@ -88,11 +90,14 @@
             device_id=dev, device_id_type=MESH,
         )
 
-    sent = []
-
-    def start(src, dst, dev, *key):
+    sent, sent_last = [], []
+
+    def start(src, dst, dev, *key, late=False):
         copy(src, dst, dev, *key).start()
-        sent.append((dst, dev, key))
+        if late:
+            sent_last.append(key)
+        else:
+            sent.append((dst, dev, key))
 
     def arrived(ref, *key):
         copy(ref, ref, right, *key).wait_recv()
@@ -162,19 +167,26 @@
         copy(stale_rows(dp_m, xp, 1 - zh), spart.at[xp], mirror, "stale").start()
     sent.append((spart, mirror, ("stale",)))
 
-    def part(k, y_):
-        return tokv.at[:, pl.ds(pl.multiple_of(k * 2048 + y_ * 512, 512), 512)]
+    def part(k, y_, rows=slice(None)):
+        return tokv.at[rows, pl.ds(pl.multiple_of(k * 2048 + y_ * 512, 512), 512)]
+
+    def rows_of(p, half):
+        return pl.ds(half * 16, 16) if p in (1, 3) else slice(None)
 
     def spread(dev, y_, *key):
+        rows = rows_of(*key[1:])
         for k in range(ZL):
-            copy(part(k, y_), tok.at[x, y, :, pl.ds(k * 512, 512)], dev, *key).start()
-        sent.append((tok.at[x, y], dev, key))
-
-    spread(at(y_=ys[1]), ys[1], "y", 1)
-    spread(at(y_=ys[3]), ys[3], "y", 3)
-    spread(right, y, "xr", 0)
-    spread(left, y, "xl", 0)
-    spread(at(y_=ys[2]), ys[2], "y", 2)
+            dst = tok.at[x, y, rows, pl.ds(k * 512, 512)]
+            copy(part(k, y_, rows), dst, dev, *key).start()
+        sent.append((tok.at[x, y, rows], dev, key))
+
+    spread(at(y_=ys[1]), ys[1], "y", 1, 0)
+    spread(at(y_=ys[3]), ys[3], "y", 3, 0)
+    spread(right, y, "xr", 0, 0)
+    spread(left, y, "xl", 0, 0)
+    spread(at(y_=ys[1]), ys[1], "y", 1, 1)
+    spread(at(y_=ys[3]), ys[3], "y", 3, 1)
+    spread(at(y_=ys[2]), ys[2], "y", 2, 0)
     for k in range(ZL):
         pltpu.make_async_copy(part(k, y), tok.at[x, y, :, pl.ds(k * 512, 512)], loc.at[6]).start()
     for dx in range(1, 4):
@@ -212,47 +224,70 @@
     for dx in (1, 3, 2):
         arrived(drecv.at[dx], "d", dx)
         merge(dx, zh, sloc)
+    def from_y(p, half=0):
+        ref = tok.at[x, ys[(4 - p) % 4], rows_of(p, half)]
+        arrived(ref, "y", p, half)
+        start(ref, ref, right, "xr", p, half)
+        start(ref, ref, left, "xl", p, half)
+
+    def token(i, p, rows=None):
+        ref = tok.at[xs[i], ys[(4 - p) % 4]]
+        return ref if rows is None else ref.at[pl.ds(rows, RB // 2), :]
+
+    def landed(i, p, name):
+        for half in range(2 if p in (1, 3) else 1):
+            arrived(tok.at[xs[i], ys[(4 - p) % 4], rows_of(p, half)], name, p, half)
+
     first_hop(0)
+    from_y(1, 0)
+    from_y(3, 0)
     arrived(spart, "stale")
     for dx in (0, 1, 3, 2):
         merge(dx, 1 - zh, spart)
     first_hop(1)
 
-    def from_y(p):
-        ref = tok.at[x, ys[(4 - p) % 4]]
-        arrived(ref, "y", p)
-        start(ref, ref, right, "xr", p)
-        start(ref, ref, left, "xl", p)
-
-    def token(i, p, rows=None):
-        ref = tok.at[xs[i], ys[(4 - p) % 4]]
-        return ref if rows is None else ref.at[pl.ds(rows, RB // 2), :]
-
-    def ring(d, hs=(0, 1)):
-        for cc in range(2 if d < 4 else 1):
-            for h in hs:
+    def ring(d):
+        for cc in range(2):
+            for h in range(2):
                 ref = block(-d, 1 - c if cc else c, h)
                 arrived(ref, "z", h, d - 1, cc)
-                if d < 3 or (d == 3 and cc == 0):
+                if d < 3:
                     start(ref, ref, onward, "z", h, d, cc)
-                start(ref, ref, sibling, "s", h, d, cc)
+                elif d == 3:
+                    last_hop(ref, h, cc)
+                start(ref, ref, sibling, "s", h, d, cc, late=d == 4)
+
+    def last_hop(ref, h, cc):
+        @pl.when(c == 1)
+        def _():
+            start(ref, ref, onward, "z", h, 3, cc, late=True)
 
     def forward(p):
         if p == 1:
-            arrived(token(3, 1), "xr", 1)
+            landed(3, 1, "xr")
             start(token(3, 1), token(3, 1), right, "fr", 1)
-            arrived(token(1, 3), "xl", 3)
+            landed(1, 3, "xl")
             start(token(1, 3), token(1, 3), left, "fl", 3)
         else:
-            arrived(token(3, p), "xr", p)
+            landed(3, p, "xr")
             start(token(3, p, 0), token(3, p, 0), right, "fr", p)
-            arrived(token(1, p), "xl", p)
+            landed(1, p, "xl")
             start(token(1, p, 16), token(1, p, 16), left, "fl", p)
 
     def siblings(d, hs=(0, 1)):
-        for cc in range(2 if d < 4 else 1):
+        for cc in range(2):
             for h in hs:
                 arrived(block(d, c if cc else 1 - c, h), "s", h, d, cc)
+
+    def last_ring():
+        @pl.when(c == 1)
+        def _():
+            ring(4)
+
+    def last_siblings(h):
+        @pl.when(c == 0)
+        def _():
+            siblings(4, (h,))
 
     def quarter(i, k):
         return wbuf[zls[i], :, :, :, halves[k]].reshape(KS // ZL, HC)
@@ -324,8 +359,8 @@
         pltpu.make_async_copy(tok.at[x, y], tok.at[x, y], loc.at[6]).wait()
 
     def near_tokens():
-        arrived(token(3, 3), "xr", 3)
-        arrived(token(1, 1), "xl", 1)
+        landed(3, 3, "xr")
+        landed(1, 1, "xl")
 
     def far_tokens():
         arrived(token(2, 1), "fr", 1)
@@ -337,8 +372,8 @@
         arrived(token(2, 0, 0), "fr", 0)
         arrived(token(2, 0, 16), "fl", 0)
 
-    from_y(1)
-    from_y(3)
+    from_y(1, 1)
+    from_y(3, 1)
     first_hop_sibling(0)
     first_hop_sibling(1)
     ring(1)
@@ -348,16 +383,15 @@
     ring(3)
     forward(2)
     forward(0)
-    ring(4, (0,))
+    last_ring()
     own_tokens()
     for d in range(1, 4):
         siblings(d)
-    ring(4, (1,))
     early(0, 0)
     near_tokens()
     early(1, 0)
     early(2, 0)
-    siblings(4, (0,))
+    last_siblings(0)
     product(0, 0)
     product(1, 0)
     product(2, 0)
@@ -365,7 +399,7 @@
         early(b, 1)
     far_tokens()
     product_far(0)
-    siblings(4, (1,))
+    last_siblings(1)
     for b in range(3):
         product(b, 1)
     product_far(1)
@@ -384,6 +418,11 @@
         ).astype(jnp.bfloat16)
     for dst, dev, key in sent:
         copy(dst, dst, dev, *key).wait_send()
+
+    @pl.when(c == 1)
+    def _():
+        for key in sent_last:
+            copy(block(4, c, 0), block(4, c, 0), sibling, *key).wait_send()
 
 
 def on_device(tokens, gain, stale, bias, first, second, grad, residual, exponent):

time: 44.3 us -> 44.1 us (level)
  no operation moved by 1% of the time
where the time goes in v6:
time: 44.1 us; the launch traced here: 43.3 us
  Pallas kernels  41.1 us (93%)
  other arithmetic  0.87 us (2%)
  local copies, waits for them, and re-layouts  0.67 us (2%)
  between operations  0.67 us (2%)
    pallas_call x1, Pallas kernels, on_device(): pl.pallas_call(kernel, out_shape=pltpu.VMEM((8, RB, HC), bf16), in_specs=...  41.1 us

profile of v6, /device:TPU:1, one launch (start us, length us, event | category | flops | bytes accessed | tf_op | source)
XLA Modules:
  0.0 43.3 jit_solution(16234460052357436249)
XLA Ops:
  0.6 0.0 copy-start
  0.6 0.0 copy-start.1
  0.7 0.0 copy-start.2
  0.7 41.1 %shard_map.112 = bf16[8,32,256]{2,1,0:T(8,128)(2,1)S(1)} custom-call(bf16[32,8192]{1,0:T(8,128)(2,1)} %tok_in.1, f32[64,128]{1,0:T(8,128)} %bitcast.4, bf16[8192,256]{1,0:T(8,128)(2,1)} %stale_ref.1, f32[1,256]{1,0:T(1,128)} %bitcast.5, f32[32,2048]{1,0:T(8,128)} %first_in.1, f32[32,2048]{1,0:T(8,128)} %second_in.1, f32[32,2048]{1,0:T(8,128)} %grad_in.1, ...), custom_call_target="tpu_custom_call" | custom-call | tf_op jit(solution)/shard_map/pallas_call | solution.py:434
  41.8 0.7 %copy.13 = bf16[256,256]{1,0:T(8,128)(2,1)} copy(bf16[256,256]{1,0:T(8,128)(2,1)S(1)} %bitcast.3) | data formatting | bytes 262144
  42.5 0.0 copy-done
  42.5 0.0 copy-done.1
  42.5 0.0 copy-done.2
  42.5 0.9 %fusion = (f32[32,2048]{1,0:T(8,128)}, f32[32,2048]{1,0:T(8,128)}) fusion(f32[32,2048]{1,0:T(8,128)S(1)} %copy-done, f32[32,2048]{1,0:T(8,128)S(1)} %copy-done.1, f32[32,2048]{1,0:T(8,128)S(1)} %copy-done.2), kind=kLoop, calls=%fused_computation.1 | loop fusion | flops 458752 | bytes 1310720 | tf_op jit(solution)/shard_map/add | solution.py:430
Async XLA Ops:
  0.6 41.8 %copy-start = (f32[32,2048]{1,0:T(8,128)S(1)}, f32[32,2048]{1,0:T(8,128)}, u32[]{:S(2)}) copy-start(f32[32,2048]{1,0:T(8,128)} %grad_in.1) | copy-start | bytes 786436
  0.6 41.8 %copy-start.1 = (f32[32,2048]{1,0:T(8,128)S(1)}, f32[32,2048]{1,0:T(8,128)}, u32[]{:S(2)}) copy-start(f32[32,2048]{1,0:T(8,128)} %second_in.1) | copy-start | bytes 786436
  0.7 41.8 %copy-start.2 = (f32[32,2048]{1,0:T(8,128)S(1)}, f32[32,2048]{1,0:T(8,128)}, u32[]{:S(2)}) copy-start(f32[32,2048]{1,0:T(8,128)} %first_in.1) | copy-start | bytes 786436
